TPU v7x, 512 devices: a whole 4x4x16 slice. The times are simulated.
512 devices in a mesh: dom: 64 (over y, z_hi, x, core), feat: 8 (over z_lo).
Axes of the slice: x: 4, y: 4, z: 16 (z_hi: 2, z_lo: 8; z = z_hi * 8 + z_lo), core: 2. Of those that a mesh axis runs over, the one named last changes fastest.
Arguments:
- features: bfloat16 [32768, 1024], P('dom', 'feat'), may hold values from -16 to 16
- weights: bfloat16 [2048, 1024], P(None, 'feat'), may hold values from -4 to 4
- send_rows: int32 [64, 64, 128], P('dom'), may hold values from -1 to 511, as said below
- remote_src: int32 [64, 64], P('dom'), may hold values from 0 to 63, each once within a row
- local_adj: bfloat16 [32768, 512], P('dom')
- remote_adj: bfloat16 [32768, 16, 128], P('dom')
- degree: int32 [32768], P('dom'), may hold values from 48 to 143
- cotangent: bfloat16 [32768, 1024], P('dom', 'feat'), may hold values from -6 to 6
Outputs:
- output: bfloat16 [32768, 1024], P('dom', 'feat')
- grad_input: bfloat16 [32768, 1024], P('dom', 'feat')
- grad_weights: float32 [2048, 1024], P('dom', 'feat')
Inputs may be any that keep to these rules, and one draw needn't show every extreme that they name: `send_rows`: each entry is a row of partition p or -1; in each block the used places come first and name distinct rows; a quarter or more of each block is used, and some block is full. `remote_src`: each row names every partition once.
All inputs are finite; a program needn't handle non-finite values.
Results may differ from a plain program's by a relative error of at most 0.01.
Values may be sent and summed in bfloat16 or wider, within the bound.
A program may use at most 64 MiB of HBM per device.

v0:
```python
import math
import jax
import jax.numpy as jnp
from jax import lax
from jax.sharding import PartitionSpec as P


def per_device(features, weights, send_rows, remote_src, local_adj, remote_adj, degree, cotangent):
    np_rows, feat_width = features.shape
    feat_count = lax.axis_size("feat")
    dom_count = lax.axis_size("dom")
    full_width = feat_width * feat_count
    tile_rows = remote_adj.shape[2]
    block_count = np_rows // tile_rows
    remote_span = remote_adj.shape[1] * tile_rows
    rows_out = send_rows[0]
    live_mask = rows_out >= 0
    safe_rows = jnp.where(live_mask, rows_out, 0)
    outgoing = jnp.where(live_mask[:, :, None], features[safe_rows], jnp.zeros((), jnp.bfloat16))
    halo_rows = lax.all_to_all(outgoing, "dom", split_axis=0, concat_axis=0, tiled=True)
    slot_order = remote_src[0]
    ordered = jnp.take(halo_rows, slot_order, axis=0).reshape(block_count, remote_span, feat_width)
    remote_tiles = remote_adj.reshape(block_count, tile_rows, remote_span)
    remote_sums = jnp.einsum(
        "bik,bkf->bif", remote_tiles, ordered, preferred_element_type=jnp.float32
    ).reshape(np_rows, feat_width)
    local_sums = jnp.dot(local_adj, features, preferred_element_type=jnp.float32)
    degree_col = degree.astype(jnp.float32)[:, None]
    aggregate = ((local_sums + remote_sums) / degree_col).astype(jnp.bfloat16)
    stacked = jnp.stack([features, aggregate], axis=1)
    weight_pair = weights.reshape(2, full_width, feat_width)
    gathered = lax.all_gather(stacked, "feat", axis=2, tiled=True)
    preact = jnp.einsum("rkc,kcf->rf", gathered, weight_pair, preferred_element_type=jnp.float32)
    output = jax.nn.silu(preact).astype(jnp.bfloat16)
    sigmoid_z = jax.nn.sigmoid(preact)
    grad_pre = (
        cotangent.astype(jnp.float32) * sigmoid_z * (1.0 + preact * (1.0 - sigmoid_z))
    ).astype(jnp.bfloat16)
    scaled_grad = (grad_pre.astype(jnp.float32) / degree_col).astype(jnp.bfloat16)
    back_ordered = jnp.einsum(
        "bik,bif->bkf",
        remote_tiles,
        scaled_grad.reshape(block_count, tile_rows, feat_width),
        preferred_element_type=jnp.float32,
    )
    back_ordered = back_ordered.reshape(slot_order.shape[0], tile_rows, feat_width).astype(
        jnp.bfloat16
    )
    returning = jnp.zeros_like(back_ordered).at[slot_order].set(back_ordered)
    arriving = lax.all_to_all(returning, "dom", split_axis=0, concat_axis=0, tiled=True)
    target_rows = jnp.where(live_mask, rows_out, np_rows).reshape(-1)
    neigh_grad = lax.dot_general(
        local_adj, scaled_grad, (((0,), (0,)), ((), ())), preferred_element_type=jnp.float32
    )
    neigh_grad = neigh_grad.at[target_rows].add(
        arriving.reshape(-1, feat_width).astype(jnp.float32), mode="drop"
    )
    neigh_grad = neigh_grad.astype(jnp.bfloat16)
    back_pair = jnp.stack([grad_pre, neigh_grad], axis=1)
    partial_terms = jnp.einsum(
        "rkf,kcf->rc", back_pair, weight_pair, preferred_element_type=jnp.float32
    )
    grad_input = lax.psum_scatter(partial_terms, "feat", scatter_dimension=1, tiled=True).astype(
        jnp.bfloat16
    )
    weight_scale = 1.0 / math.sqrt(dom_count * np_rows)
    combined = gathered.reshape(np_rows, 2 * full_width)
    summed = lax.psum_scatter(
        lax.dot_general(
            combined, grad_pre, (((0,), (0,)), ((), ())), preferred_element_type=jnp.float32
        ),
        "dom",
        scatter_dimension=0,
        tiled=True,
    )
    grad_weights = summed * weight_scale
    return (output, grad_input, grad_weights)


def solution(mesh):
    in_specs = (
        P("dom", "feat"),
        P(None, "feat"),
        P("dom", None, None),
        P("dom", None),
        P("dom", None),
        P("dom", None, None),
        P("dom"),
        P("dom", "feat"),
    )
    out_specs = (P("dom", "feat"), P("dom", "feat"), P("dom", "feat"))
    return jax.shard_map(
        per_device, mesh=mesh, in_specs=in_specs, out_specs=out_specs, check_vma=False
    )
```

profile of v0, /device:TPU:8, one launch (start us, length us, event | category | flops | bytes accessed | tf_op | source)
XLA Modules:
  0.0 959.6 jit_solution(17300601197789234725)
XLA Ops:
  7.2 0.0 copy-start
  7.2 0.8 compare_bitcast_fusion
  8.0 0.8 fusion.10
  8.8 22.8 %gather_fusion = bf16[8192,128]{1,0:T(8,128)(2,1)S(1)} fusion(bf16[512,128]{1,0:T(8,128)(2,1)} %param.8, s32[8192]{0:T(1024)S(1)} %fusion.10), kind=kCustom, calls=%fused_computation | custom fusion | bytes 4227072 | tf_op jit(solution)/shard_map/gather | solution.py:19
  31.6 2.6 broadcast_select_fusion
  34.2 0.0 copy-start.6
  34.2 0.0 copy-start.4
  34.2 21.5 %all-to-all-start = ((bf16[64,128,128]{2,1,0:T(8,128)(2,1)}), bf16[64,128,128]{2,1,0:T(8,128)(2,1)}, u32[]{:S(2)}, u32[]{:S(2)}) async-start(bf16[64,128,128]{2,1,0:T(8,128)(2,1)} %broadcast_select_fusion), calls=%async_computation | async-start | bytes 4194304 | tf_op jit(solution)/shard_map/all_to_all | solution.py:20
  55.7 0.0 all-gather.2.cloned.1.call-start
  55.8 0.5 broadcast.123
  56.3 0.0 copy-done.6
  56.3 0.7 reduce.3
  57.0 0.1 squeeze.10
  57.1 0.0 copy-done.4
  57.1 0.1 broadcast_bitcast_fusion
  57.2 2.8 reshape.130
  60.0 47.1 %all-to-all-done = bf16[64,128,128]{2,1,0:T(8,128)(2,1)} async-done(((bf16[64,128,128]{2,1,0:T(8,128)(2,1)}), bf16[64,128,128]{2,1,0:T(8,128)(2,1)}, u32[]{:S(2)}, u32[]{:S(2)}) %all-to-all-start) | async-done | bytes 2097184 | tf_op jit(solution)/shard_map/all_to_all | solution.py:20
  107.1 3.7 gather_fusion.1
  110.8 4.4 bitcast_select_fusion
  115.2 0.0 copy-start.1
  115.2 0.0 copy-start.2
  115.2 0.7 fusion.14
  115.9 0.0 copy-start.5
  115.9 0.1 copy-done.1
  116.1 0.2 copy-done.2
  116.3 0.3 fusion.5
  116.6 0.7 pad_maximum_fusion
  117.3 0.0 all-gather.2.cloned.1.call-update
  117.3 116.5 %all-gather.2.cloned.1.call-done = bf16[512,2,1024]{2,0,1:T(8,128)(2,1)} async-done(((bf16[512,2,128]{2,0,1:T(8,128)(2,1)}), bf16[512,2,1024]{2,0,1:T(8,128)(2,1)}) %all-gather.2.cloned.1.call-update) | async-done | bytes 2097168 | tf_op jit(solution)/shard_map/all_gather | solution.py:32
  233.8 0.0 copy-done
  233.8 0.0 copy-done.5
  233.8 3.0 divide_convert_fusion
  236.8 2.1 fusion.2
  238.9 3.0 copy.14
  241.9 1.8 broadcast_in_dim.39
  243.7 8.6 scatter_fusion
  252.4 9.3 all-to-all-start.1
  261.6 0.0 reduce-scatter.5.cloned.1.call-start
  261.7 3.9 copy.16
  265.6 0.0 copy-start.3
  265.6 3.3 fusion.13
  268.9 0.0 reduce-scatter.5.cloned.1.call-update
  268.9 0.0 reduce-scatter.3.cloned.1.call-start
  269.0 0.0 copy-done.3
  269.0 0.1 compare_select_fusion
  269.0 1.3 convolution_bitcast_fusion.1
  270.3 0.1 copy.15
  270.5 33.9 %all-to-all-done.1 = bf16[64,128,128]{2,1,0:T(8,128)(2,1)S(1)} async-done(((bf16[64,128,128]{2,1,0:T(8,128)(2,1)}), bf16[64,128,128]{2,1,0:T(8,128)(2,1)S(1)}, u32[]{:S(2)}, u32[]{:S(2)}) %all-to-all-start.1) | async-done | bytes 2097184 | tf_op jit(solution)/shard_map/all_to_all | solution.py:50
  304.4 44.3 %scatter_custom_fusion.1 = f32[512,128]{1,0:T(8,128)S(1)} fusion(f32[512,128]{1,0:T(8,128)S(1)} %copy.15, s32[8192]{0:T(1024)S(1)} %bitcast.73, bf16[8192,128]{1,0:T(8,128)(2,1)S(1)} %bitcast.65), kind=kCustom, calls=%fused_computation.4 | custom fusion | flops 2097152 | bytes 2359296 | tf_op jit(solution)/shard_map/scatter-add | solution.py:55
  348.7 1.8 convolution_bitcast_fusion
  350.5 0.0 reduce-scatter.3.cloned.1.call-update
  350.6 499.3 %reduce-scatter.5.cloned.1.call-done = f32[32,128]{1,0:T(8,128)} async-done(((f32[2048,128]{1,0:T(8,128)}), f32[32,128]{1,0:T(8,128)}) %reduce-scatter.5.cloned.1.call-update) | async-done | bytes 16400 | tf_op jit(solution)/shard_map/reduce_scatter | solution.py:68
  849.8 1.3 broadcast_multiply_fusion
  851.1 100.3 %reduce-scatter.3.cloned.1.call-done = f32[512,128]{1,0:T(8,128)} async-done(((f32[512,1024]{1,0:T(8,128)}), f32[512,128]{1,0:T(8,128)}) %reduce-scatter.3.cloned.1.call-update) | async-done | bytes 262160 | tf_op jit(solution)/shard_map/reduce_scatter | solution.py:63
  951.5 1.6 convert_element_type.55
  (6 shorter events, 0.0 us)
Async XLA Ops:
  7.2 226.7 %copy-start = (bf16[2048,128]{1,0:T(8,128)(2,1)S(1)}, bf16[2048,128]{1,0:T(8,128)(2,1)}, u32[]{:S(2)}) copy-start(bf16[2048,128]{1,0:T(8,128)(2,1)} %param.9) | copy-start | bytes 1572868
  34.2 22.1 %copy-start.6 = (s32[1,64]{1,0:T(1,128)S(1)}, s32[1,64]{1,0:T(1,128)}, u32[]{:S(2)}) copy-start(s32[1,64]{1,0:T(1,128)} %param.11) | copy-start | bytes 772
  34.2 22.8 %copy-start.4 = (s32[512]{0:T(512)S(1)}, s32[512]{0:T(512)}, u32[]{:S(2)}) copy-start(s32[512]{0:T(512)} %param.14) | copy-start | bytes 6148
  34.2 72.9 %all-to-all-start = ((bf16[64,128,128]{2,1,0:T(8,128)(2,1)}), bf16[64,128,128]{2,1,0:T(8,128)(2,1)}, u32[]{:S(2)}, u32[]{:S(2)}) async-start(bf16[64,128,128]{2,1,0:T(8,128)(2,1)} %broadcast_select_fusion), calls=%async_computation | async-start | bytes 4194304 | tf_op jit(solution)/shard_map/all_to_all | solution.py:20
  55.7 178.1 %all-gather.2.cloned.1.call-start = ((), (), s32[]{:S(2)}) async-start(), calls=%async_computation.4 | async-start | bytes 2359296 | tf_op jit(solution)/shard_map/all_gather | solution.py:32
  115.2 0.9 copy-start.1
  115.2 1.1 copy-start.2
  115.9 117.9 %copy-start.5 = (bf16[512,128]{1,0:T(8,128)(2,1)S(1)}, bf16[512,128]{1,0:T(8,128)(2,1)}, u32[]{:S(2)}) copy-start(bf16[512,128]{1,0:T(8,128)(2,1)} %param.15) | copy-start | bytes 393220
  252.4 52.0 %all-to-all-start.1 = ((bf16[64,128,128]{2,1,0:T(8,128)(2,1)}), bf16[64,128,128]{2,1,0:T(8,128)(2,1)S(1)}, u32[]{:S(2)}, u32[]{:S(2)}) async-start(bf16[64,128,128]{2,1,0:T(8,128)(2,1)} %scatter_fusion), calls=%async_computation.1 | async-start | bytes 4194304 | tf_op jit(solution)/shard_map/all_to_all | solution.py:50
  261.6 588.2 %reduce-scatter.5.cloned.1.call-start = ((), (), s32[]{:S(2)}) async-start(), calls=%async_computation.6 | async-start | bytes 1064960 | tf_op jit(solution)/shard_map/reduce_scatter | solution.py:68
  265.6 3.3 copy-start.3
  268.9 682.5 %reduce-scatter.3.cloned.1.call-start = ((), (), s32[]{:S(2)}) async-start(), calls=%async_computation.5 | async-start | bytes 2359296 | tf_op jit(solution)/shard_map/reduce_scatter | solution.py:63
Sparse Core Ops, SparseCore 0:
  117.5 116.3 all-gather.1
  269.0 580.7 reduce-scatter.4
  852.7 98.7 reduce-scatter.2
where the time goes:
time: 961 us; the launch traced here: 960 us
  waiting for transfers between devices  797 us (83%)
  other arithmetic  57.3 us (6%)
  local copies, waits for them, and re-layouts  47.9 us (5%)
  starting transfers between devices  30.9 us (3%)
  between operations  13.9 us (1%)
  matrix products  12.4 us (1%)
    reduce_scatter x1, waiting for transfers between devices, per_device(): lax.psum_scatter(lax.dot_general(combined, grad_pre, (((0,), (0,)), ((),...  499 us
    all_gather x1, waiting for transfers between devices, per_device(): gathered = lax.all_gather(stacked, 'feat', axis=2, tiled=True)  116 us
    reduce_scatter x1, waiting for transfers between devices, per_device(): lax.psum_scatter(partial_terms, 'feat', scatter_dimension=1, tiled=True)  100 us
    all_to_all x1, waiting for transfers between devices, per_device(): lax.all_to_all(outgoing, 'dom', split_axis=0, concat_axis=0, tiled=True)  47.1 us
    scatter-add x1, other arithmetic, per_device(): neigh_grad.at[target_rows]  44.3 us
    all_to_all x1, waiting for transfers between devices, per_device(): lax.all_to_all(returning, 'dom', split_axis=0, concat_axis=0, tiled=True)  33.9 us
    gather x1, local copies, waits for them, and re-layouts, per_device(): features[safe_rows]  22.8 us
    all_to_all x1, starting transfers between devices, per_device(): lax.all_to_all(outgoing, 'dom', split_axis=0, concat_axis=0, tiled=True)  21.5 us
  transfers between devices with their start and end apart: 5, of which 5 were waited for; matrix products, arithmetic and copies ran while one was open for 6% of the time, Pallas kernels for 0%

commit v1 on v0

--- a/solution.py
+++ b/solution.py
@@ -3,6 +3,7 @@
 import jax.numpy as jnp
 from jax import lax
 from jax.sharding import PartitionSpec as P
+from jax.lax import all_to_all, axis_size
 
 
 def per_device(features, weights, send_rows, remote_src, local_adj, remote_adj, degree, cotangent):
@@ -29,7 +30,13 @@
     aggregate = ((local_sums + remote_sums) / degree_col).astype(jnp.bfloat16)
     stacked = jnp.stack([features, aggregate], axis=1)
     weight_pair = weights.reshape(2, full_width, feat_width)
-    gathered = lax.all_gather(stacked, "feat", axis=2, tiled=True)
+    arr_next = all_to_all(
+        jnp.stack([stacked] * axis_size("feat"), axis=0),
+        axis_name="feat",
+        split_axis=0,
+        concat_axis=0,
+    )
+    gathered = jnp.concatenate(arr_next, axis=2)
     preact = jnp.einsum("rkc,kcf->rf", gathered, weight_pair, preferred_element_type=jnp.float32)
     output = jax.nn.silu(preact).astype(jnp.bfloat16)
     sigmoid_z = jax.nn.sigmoid(preact)

time: 961 us -> 1010 us (1.051)
  blocking collectives: 0 us -> 154 us
  waiting for transfers between devices: 797 us -> 692 us
    all_to_all x0 -> x1, blocking collectives: none -> 154 us  [per_device(): all_to_all(jnp.stack([stacked] * axis_size('feat'), axis=0), axis_name='f...]
    all_gather x1 -> x0, waiting for transfers between devices: 116 us -> none  [per_device(): gathered = lax.all_gather(stacked, 'feat', axis=2, tiled=True)]
    reduce_scatter x1, waiting for transfers between devices: 499 us -> 426 us  [per_device(): lax.psum_scatter(lax.dot_general(combined, grad_pre, (((0,), (0,)), ((),...]
    all_to_all x1, waiting for transfers between devices: 33.9 us -> 95.3 us  [per_device(): lax.all_to_all(returning, 'dom', split_axis=0, concat_axis=0, tiled=True)]
    reduce_scatter x1, waiting for transfers between devices: 100 us -> 124 us  [per_device(): lax.psum_scatter(partial_terms, 'feat', scatter_dimension=1, tiled=True)]
  transfers between devices with their start and end apart: 5 -> 4, of which waited for: 5 -> 4; matrix products, arithmetic and copies ran while one was open for 6% -> 5% of each run, Pallas kernels for 0% -> 0%
where the time goes in v1:
time: 1010 us
  waiting for transfers between devices  692 us (69%)
  blocking collectives  154 us (15%)
  other arithmetic  57 us (6%)
  local copies, waits for them, and re-layouts  53.2 us (5%)
  starting transfers between devices  28.1 us (3%)
  between operations  14.3 us (1%)
    reduce_scatter x1, waiting for transfers between devices, per_device(): lax.psum_scatter(lax.dot_general(combined, grad_pre, (((0,), (0,)), ((),...  426 us
    all_to_all x1, blocking collectives, per_device(): all_to_all(jnp.stack([stacked] * axis_size('feat'), axis=0), axis_name='f...  154 us
    reduce_scatter x1, waiting for transfers between devices, per_device(): lax.psum_scatter(partial_terms, 'feat', scatter_dimension=1, tiled=True)  124 us
    all_to_all x1, waiting for transfers between devices, per_device(): lax.all_to_all(returning, 'dom', split_axis=0, concat_axis=0, tiled=True)  95.3 us
    all_to_all x1, waiting for transfers between devices, per_device(): lax.all_to_all(outgoing, 'dom', split_axis=0, concat_axis=0, tiled=True)  47.1 us
    scatter-add x1, other arithmetic, per_device(): neigh_grad.at[target_rows]  44.7 us
    gather x1, local copies, waits for them, and re-layouts, per_device(): features[safe_rows]  22.8 us
    all_to_all x1, starting transfers between devices, per_device(): lax.all_to_all(outgoing, 'dom', split_axis=0, concat_axis=0, tiled=True)  21.5 us
  transfers between devices with their start and end apart: 4, of which 4 were waited for; matrix products, arithmetic and copies ran while one was open for 5% of the time, Pallas kernels for 0%

profile of v1, /device:TPU:8, one launch (start us, length us, event | category | flops | bytes accessed | tf_op | source)
XLA Modules:
  0.0 1008.3 jit_solution(18170420146231371856)
XLA Ops:
  7.2 0.0 copy-start
  7.2 0.8 compare_bitcast_fusion
  8.0 0.8 fusion.10
  8.8 22.8 %gather_fusion = bf16[8192,128]{1,0:T(8,128)(2,1)S(1)} fusion(bf16[512,128]{1,0:T(8,128)(2,1)} %param.8, s32[8192]{0:T(1024)S(1)} %fusion.10), kind=kCustom, calls=%fused_computation | custom fusion | bytes 4227072 | tf_op jit(solution)/shard_map/gather | solution.py:20
  31.6 2.7 broadcast_select_fusion
  34.2 0.0 copy-start.8
  34.2 0.0 copy-start.6
  34.2 21.5 %all-to-all-start = ((bf16[64,128,128]{2,1,0:T(8,128)(2,1)}), bf16[64,128,128]{2,1,0:T(8,128)(2,1)}, u32[]{:S(2)}, u32[]{:S(2)}) async-start(bf16[64,128,128]{2,1,0:T(8,128)(2,1)} %broadcast_select_fusion), calls=%async_computation | async-start | bytes 4194304 | tf_op jit(solution)/shard_map/all_to_all | solution.py:21
  55.8 0.5 broadcast.125
  56.3 0.0 copy-done.8
  56.3 0.7 reduce.3
  56.9 0.1 squeeze.10
  57.0 0.0 copy-done.6
  57.0 0.1 broadcast_bitcast_fusion
  57.1 2.8 reshape.135
  60.0 47.1 %all-to-all-done = bf16[64,128,128]{2,1,0:T(8,128)(2,1)} async-done(((bf16[64,128,128]{2,1,0:T(8,128)(2,1)}), bf16[64,128,128]{2,1,0:T(8,128)(2,1)}, u32[]{:S(2)}, u32[]{:S(2)}) %all-to-all-start) | async-done | bytes 2097184 | tf_op jit(solution)/shard_map/all_to_all | solution.py:21
  107.1 3.7 gather_fusion.1
  110.8 4.4 bitcast_select_fusion
  115.2 0.0 copy-start.1
  115.2 0.0 copy-start.3
  115.2 0.7 fusion.14
  116.0 0.1 copy-done.1
  116.1 0.2 copy-done.3
  116.3 0.3 fusion.5
  116.6 0.1 copy.18
  116.8 0.2 stack.32
  117.0 153.7 %all_to_all.15 = bf16[8,512,2,128]{1,3,2,0:T(8,128)(2,1)} all-to-all(bf16[8,512,2,128]{1,3,2,0:T(8,128)(2,1)S(1)} %stack.32), channel_id=1, replica_groups=mesh['dom'=64,'feat'=8] {'feat'}, dimensions={0} | all-to-all | bytes 4194304 | tf_op jit(solution)/shard_map/all_to_all | solution.py:33
  270.7 4.3 copy.20
  275.0 0.0 copy-start.7
  275.0 4.2 reshape.138
  279.2 0.0 copy-done
  279.2 0.0 copy-done.7
  279.2 3.0 divide_convert_fusion
  282.2 2.1 fusion.2
  284.3 3.0 copy.22
  287.3 1.8 broadcast_in_dim.39
  289.1 8.7 scatter_fusion
  297.8 0.0 copy-start.2
  297.8 6.6 all-to-all-start.2
  304.4 0.0 reduce-scatter.5.cloned.1.call-start
  304.5 0.0 copy-done.2
  304.5 0.2 copy.19
  304.7 0.0 copy-start.5
  304.7 0.0 copy-start.4
  304.7 1.7 fusion.13
  306.4 0.0 reduce-scatter.5.cloned.1.call-update
  306.4 0.0 reduce-scatter.3.cloned.1.call-start
  306.5 0.0 copy-done.5
  306.5 0.1 compare_select_fusion
  306.5 0.0 copy-done.4
  306.5 0.2 convolution_bitcast_fusion.1
  306.8 0.1 copy.23
  306.9 95.3 %all-to-all-done.2 = bf16[64,128,128]{2,1,0:T(8,128)(2,1)} async-done(((bf16[64,128,128]{2,1,0:T(8,128)(2,1)}), bf16[64,128,128]{2,1,0:T(8,128)(2,1)}, u32[]{:S(2)}, u32[]{:S(2)}) %all-to-all-start.2) | async-done | bytes 2097184 | tf_op jit(solution)/shard_map/all_to_all | solution.py:57
  402.2 44.7 %scatter_custom_fusion.1 = f32[512,128]{1,0:T(8,128)S(1)} fusion(f32[512,128]{1,0:T(8,128)S(1)} %copy.23, s32[8192]{0:T(1024)S(1)} %bitcast.80, bf16[8192,128]{1,0:T(8,128)(2,1)} %bitcast.27), kind=kCustom, calls=%fused_computation.4 | custom fusion | flops 2097152 | bytes 2359296 | tf_op jit(solution)/shard_map/scatter-add | solution.py:62
  446.9 1.8 convolution_bitcast_fusion
  448.8 0.0 reduce-scatter.3.cloned.1.call-update
  448.8 425.9 %reduce-scatter.5.cloned.1.call-done = f32[32,128]{1,0:T(8,128)} async-done(((f32[2048,128]{1,0:T(8,128)}), f32[32,128]{1,0:T(8,128)}) %reduce-scatter.5.cloned.1.call-update) | async-done | bytes 16400 | tf_op jit(solution)/shard_map/reduce_scatter | solution.py:75
  874.7 1.3 broadcast_multiply_fusion
  876.0 123.8 %reduce-scatter.3.cloned.1.call-done = f32[512,128]{1,0:T(8,128)} async-done(((f32[512,1024]{1,0:T(8,128)}), f32[512,128]{1,0:T(8,128)}) %reduce-scatter.3.cloned.1.call-update) | async-done | bytes 262160 | tf_op jit(solution)/shard_map/reduce_scatter | solution.py:70
  999.8 1.6 convert_element_type.55
  (7 shorter events, 0.1 us)
Async XLA Ops:
  7.2 272.1 %copy-start = (bf16[2048,128]{1,0:T(8,128)(2,1)S(1)}, bf16[2048,128]{1,0:T(8,128)(2,1)}, u32[]{:S(2)}) copy-start(bf16[2048,128]{1,0:T(8,128)(2,1)} %param.9) | copy-start | bytes 1572868
  34.2 22.0 %copy-start.8 = (s32[1,64]{1,0:T(1,128)S(1)}, s32[1,64]{1,0:T(1,128)}, u32[]{:S(2)}) copy-start(s32[1,64]{1,0:T(1,128)} %param.11) | copy-start | bytes 772
  34.2 22.8 %copy-start.6 = (s32[512]{0:T(512)S(1)}, s32[512]{0:T(512)}, u32[]{:S(2)}) copy-start(s32[512]{0:T(512)} %param.14) | copy-start | bytes 6148
  34.2 72.9 %all-to-all-start = ((bf16[64,128,128]{2,1,0:T(8,128)(2,1)}), bf16[64,128,128]{2,1,0:T(8,128)(2,1)}, u32[]{:S(2)}, u32[]{:S(2)}) async-start(bf16[64,128,128]{2,1,0:T(8,128)(2,1)} %broadcast_select_fusion), calls=%async_computation | async-start | bytes 4194304 | tf_op jit(solution)/shard_map/all_to_all | solution.py:21
  115.2 0.9 copy-start.1
  115.2 1.1 copy-start.3
  275.0 4.2 copy-start.7
  297.8 6.6 copy-start.2
  297.8 104.4 %all-to-all-start.2 = ((bf16[64,128,128]{2,1,0:T(8,128)(2,1)}), bf16[64,128,128]{2,1,0:T(8,128)(2,1)}, u32[]{:S(2)}, u32[]{:S(2)}) async-start(bf16[64,128,128]{2,1,0:T(8,128)(2,1)} %scatter_fusion), calls=%async_computation.2 | async-start | bytes 4194304 | tf_op jit(solution)/shard_map/all_to_all | solution.py:57
  304.4 570.3 %reduce-scatter.5.cloned.1.call-start = ((), (), s32[]{:S(2)}) async-start(), calls=%async_computation.6 | async-start | bytes 1064960 | tf_op jit(solution)/shard_map/reduce_scatter | solution.py:75
  304.7 1.8 copy-start.5
  304.7 1.8 copy-start.4
  306.4 693.4 %reduce-scatter.3.cloned.1.call-start = ((), (), s32[]{:S(2)}) async-start(), calls=%async_computation.5 | async-start | bytes 2359296 | tf_op jit(solution)/shard_map/reduce_scatter | solution.py:70
Sparse Core Ops, SparseCore 0:
  308.0 566.6 reduce-scatter.4
  877.6 122.1 reduce-scatter.2
